TPU v7x, 32 devices: a whole 2x2x4 slice. The times are simulated.
32 devices in a mesh: groups: 2 (over x), weight: 16 (over z, y, core).
Axes of the slice: x: 2, y: 2, z: 4, core: 2. Of those that a mesh axis runs over, the one named last changes fastest.
Arguments:
- hidden: bfloat16 [128, 8192], P(('groups', 'weight')), parts along dimension 0, may hold values from -6 to 6
- norm_gain: float32 [8192], replicated, may hold values from 0.1 to 1.9
- in_weight: bfloat16 [8192, 2, 8192], P(None, None, 'weight'), may hold values from -0.0625 to 0.0625
- conv_weight: float32 [4, 8192], P(None, 'weight'), may hold values from -0.6 to 0.6
- conv_offset: float32 [8192], P('weight'), may hold values from -0.5 to 0.5
- coef_weight: bfloat16 [8192, 544], P('weight'), may hold values from -0.0625 to 0.0625
- step_weight: bfloat16 [512, 8192], P(None, 'weight'), may hold values from -0.25 to 0.25
- step_bias: float32 [8192], P('weight'), may hold values from -3 to 0.5
- log_rates: float32 [16, 8192], P(None, 'weight'), may hold values from 0 to 2.77
- skip_gain: float32 [8192], P('weight'), may hold values from 0.5 to 1.5
- out_weight: bfloat16 [8192, 8192], P('weight'), may hold values from -0.0625 to 0.0625
- ssm_state: bfloat16 [128, 16, 8192], P('groups', None, 'weight'), parts along dimension 0, may hold values from -6 to 6
- conv_state: bfloat16 [128, 3, 8192], P('groups', None, 'weight'), parts along dimension 0, may hold values from -6 to 6
- live_counts: int32 [32], P('groups'), parts along dimension 0, may hold values from 1 to 3, as said below
Outputs:
- mixed: bfloat16 [128, 8192], P(('groups', 'weight')), parts along dimension 0
- new_state: bfloat16 [128, 16, 8192], P('groups', None, 'weight'), parts along dimension 0
- new_conv: bfloat16 [128, 3, 8192], P('groups', None, 'weight'), parts along dimension 0
There are 2 independent parts, one for each index of `groups`. A program takes and returns all parts, laid end to end along the dimension named above; an argument that names none is the same for every part. Nothing has to cross between parts.
Inputs may be any that keep to these rules, and one draw needn't show every extreme that they name: The live rows of a microbatch are its first live_counts rows; the most, 3, is reached by some microbatch.
All inputs are finite; a program needn't handle non-finite values.
Results may differ from a plain program's by a relative error of at most 0.0039.
Values may be sent and summed in bfloat16 or wider, within the bound.
A program may use at most 64 MiB of HBM per device.

v0:
```python
import jax
import jax.numpy as jnp
from jax import lax
from jax.sharding import PartitionSpec as P

NSTATE = 16
DTR = 512
LIVE_MAX = 3


def rms_normed(hidden, norm_gain):
    wide = hidden.astype(jnp.float32)
    factor = lax.rsqrt(jnp.mean(wide * wide, axis=-1, keepdims=True) + 1e-05)
    return (wide * factor * norm_gain).astype(jnp.bfloat16)


def body(
    hidden,
    norm_gain,
    in_weight,
    conv_weight,
    conv_offset,
    coef_weight,
    step_weight,
    step_bias,
    log_rates,
    skip_gain,
    out_weight,
    ssm_state,
    conv_state,
    live_counts,
):
    devices = lax.axis_size("weight")
    rows_dev = hidden.shape[0]
    channels = in_weight.shape[2]
    states_n = ssm_state.shape[1]
    kept = LIVE_MAX
    normed = rms_normed(hidden[:kept], norm_gain)
    joined = in_weight.reshape(in_weight.shape[0], 2 * channels)
    both = jnp.dot(
        lax.all_gather(normed, "weight", axis=0, tiled=True),
        joined,
        preferred_element_type=jnp.float32,
    )
    total_rows = both.shape[0]
    conv_input = both[:, :channels].astype(jnp.bfloat16)
    gate_branch = both[:, channels:]
    state_grid = ssm_state.reshape(devices, rows_dev, states_n, channels)
    conv_grid = conv_state.reshape(devices, rows_dev, 3, channels)
    state_kept = state_grid[:, :kept].reshape(total_rows, states_n, channels)
    conv_kept = conv_grid[:, :kept].reshape(total_rows, 3, channels)
    row_ids = jnp.arange(total_rows, dtype=jnp.int32)
    per_row = jnp.repeat(live_counts, kept, total_repeat_length=total_rows)
    alive = row_ids % kept < per_row
    window = jnp.concatenate([conv_kept, conv_input[:, None, :]], axis=1)
    convolved = jnp.sum(window.astype(jnp.float32) * conv_weight[None], axis=1) + conv_offset
    mixed_x = jax.nn.silu(convolved).astype(jnp.bfloat16)
    partial_low = jnp.dot(mixed_x, coef_weight, preferred_element_type=jnp.float32)
    low_rank = lax.psum(partial_low, "weight")
    step_low = low_rank[:, :DTR].astype(jnp.bfloat16)
    in_coef = low_rank[:, DTR : DTR + NSTATE]
    out_coef = low_rank[:, DTR + NSTATE :]
    step_size = jax.nn.softplus(
        jnp.dot(step_low, step_weight, preferred_element_type=jnp.float32) + step_bias
    )
    x_wide = mixed_x.astype(jnp.float32)
    decays = jnp.exp(-step_size[:, None, :] * jnp.exp(log_rates)[None])
    old_state = state_kept.astype(jnp.float32)
    updated = decays * old_state + step_size[:, None, :] * in_coef[:, :, None] * x_wide[:, None, :]
    readout = jnp.sum(out_coef[:, :, None] * updated, axis=1) + skip_gain * x_wide
    gated_out = jnp.where(alive[:, None], readout * jax.nn.silu(gate_branch), 0.0).astype(
        jnp.bfloat16
    )
    block = lax.slice_in_dim(gated_out, 0, lax.axis_size("weight") * kept, axis=0)
    mixer_term = lax.psum_scatter(
        jnp.dot(block, out_weight, preferred_element_type=jnp.float32),
        "weight",
        scatter_dimension=0,
        tiled=True,
    )
    own_mixed = (hidden[:kept].astype(jnp.float32) + mixer_term).astype(jnp.bfloat16)
    mixed = jnp.concatenate([own_mixed, hidden[kept:]], axis=0)
    state_new_kept = jnp.where(alive[:, None, None], updated, old_state).astype(jnp.bfloat16)
    conv_new_kept = jnp.where(alive[:, None, None], window[:, 1:], conv_kept)
    new_state = jnp.concatenate(
        [state_new_kept.reshape(devices, kept, states_n, channels), state_grid[:, kept:]], axis=1
    ).reshape(ssm_state.shape)
    new_conv = jnp.concatenate(
        [conv_new_kept.reshape(devices, kept, 3, channels), conv_grid[:, kept:]], axis=1
    ).reshape(conv_state.shape)
    return (mixed, new_state, new_conv)


def solution(mesh):
    in_specs = (
        P(("groups", "weight"), None),
        P(),
        P(None, None, "weight"),
        P(None, "weight"),
        P("weight"),
        P("weight", None),
        P(None, "weight"),
        P("weight"),
        P(None, "weight"),
        P("weight"),
        P("weight", None),
        P("groups", None, "weight"),
        P("groups", None, "weight"),
        P("groups"),
    )
    out_specs = (
        P(("groups", "weight"), None),
        P("groups", None, "weight"),
        P("groups", None, "weight"),
    )
    return jax.shard_map(body, mesh=mesh, in_specs=in_specs, out_specs=out_specs, check_vma=False)
```

profile of v0, /device:TPU:0, one launch (start us, length us, event | category | flops | bytes accessed | tf_op | source)
XLA Modules:
  0.0 255.2 jit_solution(7793074444627123706)
XLA Ops:
  7.2 1.1 fusion.4
  8.3 1.0 fusion.8
  9.3 26.3 %all-gather = bf16[16,3,8192]{2,1,0:T(4,128)(2,1)S(1)} all-gather(bf16[1,3,8192]{2,1,0:T(4,128)(2,1)S(1)} %fusion.8), channel_id=1, replica_groups=mesh['groups'=2,'weight'=16] {'weight'}, dimensions={0}, use_global_device_ids=true | all-gather | bytes 835584 | tf_op jit(solution)/shard_map/all_gather | solution.py:41
  35.5 0.7 reshape.164
  36.2 11.4 %copy.19 = bf16[1024,8,2,512]{3,1,2,0:T(8,128)(2,1)S(1)} copy(bf16[1024,8,2,512]{3,2,1,0:T(2,128)(2,1)} %bitcast.24) | data formatting | bytes 33554432
  47.7 3.1 %fusion.26 = f32[48,1024]{1,0:T(8,128)S(1)} fusion(bf16[48,8192]{1,0:T(8,128)(2,1)S(1)} %reshape.164, bf16[8192,1024]{1,0:T(8,128)(2,1)S(1)} %bitcast.23), kind=kOutput, calls=%fused_computation.53 | convolution fusion | flops 805306368 | bytes 17760256 | tf_op jit(solution)/shard_map/dot_general | solution.py:40
  50.9 0.1 reshape.149
  51.1 0.9 fusion.23
  52.3 0.8 gather_fusion
  53.1 0.1 gather.7
  53.1 0.6 fusion.16
  53.8 0.6 fusion.20
  54.3 0.1 copy.18
  54.4 0.6 exp.27
  55.1 81.9 %all-reduce.4.cloned.1.call-done = f32[48,544]{1,0:T(8,128)} async-done(((f32[48,544]{1,0:T(8,128)}), f32[48,544]{1,0:T(8,128)}) %all-reduce.4.cloned.1.call-update) | async-done | bytes 104464 | tf_op jit(solution)/shard_map/psum | solution.py:59
  137.0 0.9 fusion.24
  137.9 0.6 mul.130
  138.5 1.1 fusion.25
  139.8 0.6 mul.121
  140.4 1.7 fusion.1
  142.2 6.2 %fusion.9 = f32[48,8192]{1,0:T(8,128)} fusion(bf16[512,8192]{1,0:T(8,128)(2,1)} %param.26, f32[48,1024]{1,0:T(8,128)S(1)} %fusion.26, f32[48,512]{1,0:T(8,128)S(1)} %reduce_sum.35, f32[512]{0:T(512)} %param.25, pred[48]{0:T(512)(128)(4,1)} %fusion.20, f32[48,512]{1,0:T(8,128)S(1)} %multiply_reduce_fusion.1, f32[512]{0:T(512)} %param.20), kind=kOutput, calls=%fused_computation.31 | convolution fusion | flops 403046400 | bytes 10260528 | tf_op jit(solution)/shard_map/dot_general | solution.py:76
  148.4 0.8 copy-done.3
  149.3 0.1 slice.76
  149.4 0.1 fusion.3
  149.5 0.1 reshape.153
  149.6 0.2 pad_maximum_fusion.2
  149.8 0.7 reshape.154
  150.6 0.6 dynamic-slice.6
  151.8 1.1 pad_maximum_fusion
  152.9 93.7 %all-reduce.6.cloned.1.call-done = f32[48,8192]{1,0:T(8,128)} async-done(((f32[48,8192]{1,0:T(8,128)}), f32[48,8192]{1,0:T(8,128)}) %all-reduce.6.cloned.1.call-update) | async-done | bytes 1572880
  246.6 1.1 fusion.7
  247.7 0.7 pad_maximum_fusion.3
  (45 shorter events, 0.6 us)
Async XLA Ops:
  7.2 43.9 %copy-start = (bf16[512,544]{0,1:T(8,128)(2,1)S(1)}, bf16[512,544]{0,1:T(8,128)(2,1)}, u32[]{:S(2)}) copy-start(bf16[512,544]{0,1:T(8,128)(2,1)} %param.21) | copy-start | bytes 1671172
  7.2 129.8 %all-reduce.4.cloned.1.call-start = ((), (), s32[]{:S(2)}) async-start(), calls=%async_computation | async-start | bytes 245760 | tf_op jit(solution)/shard_map/psum | solution.py:59
  47.6 3.2 %copy-start.7 = (bf16[64,3,512]{2,0,1:T(8,128)(2,1)S(1)}, bf16[64,3,512]{2,0,1:T(8,128)(2,1)}, u32[]{:S(2)}) copy-start(bf16[64,3,512]{2,0,1:T(8,128)(2,1)} %param.28) | copy-start | bytes 589828
  47.6 3.4 %copy-start.10 = (f32[4,512]{1,0:T(4,128)S(1)}, f32[4,512]{1,0:T(4,128)}, u32[]{:S(2)}) copy-start(f32[4,512]{1,0:T(4,128)} %param.19) | copy-start | bytes 24580
  47.7 3.5 %copy-start.8 = (f32[512]{0:T(512)S(1)}, f32[512]{0:T(512)}, u32[]{:S(2)}) copy-start(f32[512]{0:T(512)} %param.20) | copy-start | bytes 6148
  50.8 1.5 copy-start.13
  50.8 1.5 copy-start.1
  50.8 3.6 %copy-start.5 = (bf16[48,1,512]{2,0,1:T(8,128)(2,1)}, bf16[48,1,512]{2,0,1:T(8,128)(2,1)S(1)}, u32[]{:S(2)}) copy-start(bf16[48,1,512]{2,0,1:T(8,128)(2,1)S(1)} %fusion.10) | copy-start | bytes 147460
  50.8 3.6 %copy-start.9 = (f32[16,512]{1,0:T(8,128)S(1)}, f32[16,512]{1,0:T(8,128)}, u32[]{:S(2)}) copy-start(f32[16,512]{1,0:T(8,128)} %param.24) | copy-start | bytes 98308
  50.9 87.6 %copy-start.4 = (bf16[512,512]{1,0:T(8,128)(2,1)S(1)}, bf16[512,512]{1,0:T(8,128)(2,1)}, u32[]{:S(2)}) copy-start(bf16[512,512]{1,0:T(8,128)(2,1)} %param.22) | copy-start | bytes 1572868
  50.9 87.6 %copy-start.12 = (f32[512]{0:T(512)S(1)}, f32[512]{0:T(512)}, u32[]{:S(2)}) copy-start(f32[512]{0:T(512)} %param.23) | copy-start | bytes 6148
  52.1 88.3 %copy-start.2 = (bf16[64,16,512]{2,1,0:T(8,128)(2,1)S(1)}, bf16[64,16,512]{2,1,0:T(8,128)(2,1)}, u32[]{:S(2)}) copy-start(bf16[64,16,512]{2,1,0:T(8,128)(2,1)} %param.27) | copy-start | bytes 3145732
  52.1 194.5 %all-reduce.6.cloned.1.call-start = ((), (), s32[]{:S(2)}) async-start(), calls=%async_computation.1 | async-start | bytes 3145728
  148.4 0.8 copy-start.3
  148.4 1.0 copy-start.6
  148.4 1.0 copy-start.11
  149.2 1.3 copy-start.14
Sparse Core Ops, SparseCore 0:
  52.2 84.7 all-reduce.3
  148.5 98.0 all-reduce.5
where the time goes:
time: 256 us; the launch traced here: 255 us
  waiting for transfers between devices  176 us (69%)
  blocking collectives  26.3 us (10%)
  local copies, waits for them, and re-layouts  18.6 us (7%)
  between operations  15 us (6%)
  matrix products  11.3 us (4%)
  other arithmetic  8.21 us (3%)
    unnamed x3, waiting for transfers between devices  93.8 us
    psum x1, waiting for transfers between devices, body(): low_rank = lax.psum(partial_low, 'weight')  81.9 us
    all_gather x1, blocking collectives, body(): lax.all_gather(normed, 'weight', axis=0, tiled=True)  26.3 us
    unnamed x33, local copies, waits for them, and re-layouts  13.6 us
    dot_general x1, matrix products, body(): jnp.dot(block, out_weight, preferred_element_type=jnp.float32)  6.19 us
  transfers between devices with their start and end apart: 2, of which 2 were waited for; matrix products, arithmetic and copies ran while one was open for 2% of the time, Pallas kernels for 0%

commit v1 on v0

--- a/solution.py
+++ b/solution.py
@@ -2,6 +2,7 @@
 import jax.numpy as jnp
 from jax import lax
 from jax.sharding import PartitionSpec as P
+from jax.lax import all_gather
 
 NSTATE = 16
 DTR = 512
@@ -56,7 +57,8 @@
     convolved = jnp.sum(window.astype(jnp.float32) * conv_weight[None], axis=1) + conv_offset
     mixed_x = jax.nn.silu(convolved).astype(jnp.bfloat16)
     partial_low = jnp.dot(mixed_x, coef_weight, preferred_element_type=jnp.float32)
-    low_rank = lax.psum(partial_low, "weight")
+    y = all_gather(partial_low, axis_name="weight")
+    low_rank = jnp.sum(y, axis=0)
     step_low = low_rank[:, :DTR].astype(jnp.bfloat16)
     in_coef = low_rank[:, DTR : DTR + NSTATE]
     out_coef = low_rank[:, DTR + NSTATE :]

time: 256 us -> 206 us (0.80)
  waiting for transfers between devices: 176 us -> 126 us
    psum x1 -> x0, waiting for transfers between devices: 81.9 us -> none  [body(): low_rank = lax.psum(partial_low, 'weight')]
    all_gather x0 -> x1, waiting for transfers between devices: none -> 35.4 us  [body(): y = all_gather(partial_low, axis_name='weight')]
    unnamed x3, waiting for transfers between devices: 93.8 us -> 90.2 us
  transfers between devices with their start and end apart: 2 -> 2, of which waited for: 2 -> 2; matrix products, arithmetic and copies ran while one was open for 2% -> 3% of each run, Pallas kernels for 0% -> 0%
where the time goes in v1:
time: 206 us; the launch traced here: 205 us
  waiting for transfers between devices  126 us (61%)
  blocking collectives  26.3 us (13%)
  local copies, waits for them, and re-layouts  17.8 us (9%)
  between operations  15 us (7%)
  matrix products  10.5 us (5%)
  other arithmetic  9.95 us (5%)
    unnamed x3, waiting for transfers between devices  90.2 us
    all_gather x1, waiting for transfers between devices, body(): y = all_gather(partial_low, axis_name='weight')  35.4 us
    all_gather x1, blocking collectives, body(): lax.all_gather(normed, 'weight', axis=0, tiled=True)  26.3 us
    unnamed x33, local copies, waits for them, and re-layouts  13.6 us
    dot_general x1, matrix products, body(): jnp.dot(block, out_weight, preferred_element_type=jnp.float32)  6.19 us
  transfers between devices with their start and end apart: 2, of which 2 were waited for; matrix products, arithmetic and copies ran while one was open for 3% of the time, Pallas kernels for 0%

profile of v1, /device:TPU:0, one launch (start us, length us, event | category | flops | bytes accessed | tf_op | source)
XLA Modules:
  0.0 205.2 jit_solution(17757245868268286427)
XLA Ops:
  7.2 1.1 fusion.4
  8.3 1.0 fusion.8
  9.3 26.3 %all-gather.1 = bf16[16,3,8192]{2,1,0:T(4,128)(2,1)S(1)} all-gather(bf16[1,3,8192]{2,1,0:T(4,128)(2,1)S(1)} %fusion.8), channel_id=1, replica_groups=mesh['groups'=2,'weight'=16] {'weight'}, dimensions={0}, use_global_device_ids=true | all-gather | bytes 835584 | tf_op jit(solution)/shard_map/all_gather | solution.py:42
  35.5 0.7 reshape.165
  36.2 11.4 %copy.19 = bf16[1024,8,2,512]{3,1,2,0:T(8,128)(2,1)S(1)} copy(bf16[1024,8,2,512]{3,2,1,0:T(2,128)(2,1)} %bitcast.25) | data formatting | bytes 33554432
  47.7 3.1 %fusion.26 = f32[48,1024]{1,0:T(8,128)S(1)} fusion(bf16[48,8192]{1,0:T(8,128)(2,1)S(1)} %reshape.165, bf16[8192,1024]{1,0:T(8,128)(2,1)S(1)} %bitcast.24), kind=kOutput, calls=%fused_computation.53 | convolution fusion | flops 805306368 | bytes 17760256 | tf_op jit(solution)/shard_map/dot_general | solution.py:41
  50.9 0.1 reshape.149
  51.1 0.9 fusion.23
  52.3 0.6 exp.27
  53.0 0.8 gather_fusion
  53.8 0.1 gather.7
  53.8 0.6 fusion.20
  54.4 0.6 fusion.16
  55.0 35.4 %all-gather.4.cloned.1.call-done = f32[768,544]{1,0:T(8,128)} async-done(((f32[48,544]{1,0:T(8,128)}), f32[768,544]{1,0:T(8,128)}) %all-gather.4.cloned.1.call-update) | async-done | bytes 1671184 | tf_op jit(solution)/shard_map/all_gather | solution.py:60
  90.5 1.7 reduce_sum.42
  92.2 0.1 fusion.24
  92.3 0.6 mul.130
  93.0 0.3 fusion.25
  93.3 0.6 mul.121
  93.9 1.7 fusion.1
  95.7 6.2 %fusion.9 = f32[48,8192]{1,0:T(8,128)} fusion(bf16[512,8192]{1,0:T(8,128)(2,1)} %param.26, f32[48,1024]{1,0:T(8,128)S(1)} %fusion.26, f32[48,512]{1,0:T(8,128)S(1)} %reduce_sum.45, f32[512]{0:T(512)} %param.25, pred[48]{0:T(512)(128)(4,1)} %fusion.20, f32[48,512]{1,0:T(8,128)S(1)} %multiply_reduce_fusion.1, f32[512]{0:T(512)} %param.20), kind=kOutput, calls=%fused_computation.31 | convolution fusion | flops 403046400 | bytes 10260528 | tf_op jit(solution)/shard_map/dot_general | solution.py:78
  101.9 0.8 copy-done.3
  102.8 0.1 slice.76
  103.0 0.1 fusion.3
  103.0 0.1 reshape.153
  103.1 0.2 pad_maximum_fusion.2
  103.4 0.7 reshape.154
  104.1 0.6 dynamic-slice.6
  105.3 1.1 pad_maximum_fusion
  106.4 90.2 %all-reduce.3.cloned.1.call-done = f32[48,8192]{1,0:T(8,128)} async-done(((f32[48,8192]{1,0:T(8,128)}), f32[48,8192]{1,0:T(8,128)}) %all-reduce.3.cloned.1.call-update) | async-done | bytes 1572880
  196.6 1.1 fusion.7
  197.7 0.7 pad_maximum_fusion.3
  (46 shorter events, 0.7 us)
Async XLA Ops:
  7.2 43.9 %copy-start = (bf16[512,544]{0,1:T(8,128)(2,1)S(1)}, bf16[512,544]{0,1:T(8,128)(2,1)}, u32[]{:S(2)}) copy-start(bf16[512,544]{0,1:T(8,128)(2,1)} %param.21) | copy-start | bytes 1671172
  7.2 83.3 %all-gather.4.cloned.1.call-start = ((), (), s32[]{:S(2)}) async-start(), calls=%async_computation | async-start | bytes 2088960 | tf_op jit(solution)/shard_map/all_gather | solution.py:60
  47.6 3.2 %copy-start.7 = (bf16[64,3,512]{2,0,1:T(8,128)(2,1)S(1)}, bf16[64,3,512]{2,0,1:T(8,128)(2,1)}, u32[]{:S(2)}) copy-start(bf16[64,3,512]{2,0,1:T(8,128)(2,1)} %param.28) | copy-start | bytes 589828
  47.6 3.4 %copy-start.10 = (f32[4,512]{1,0:T(4,128)S(1)}, f32[4,512]{1,0:T(4,128)}, u32[]{:S(2)}) copy-start(f32[4,512]{1,0:T(4,128)} %param.19) | copy-start | bytes 24580
  47.7 3.4 %copy-start.8 = (f32[512]{0:T(512)S(1)}, f32[512]{0:T(512)}, u32[]{:S(2)}) copy-start(f32[512]{0:T(512)} %param.20) | copy-start | bytes 6148
  50.8 1.6 copy-start.9
  50.8 2.2 %copy-start.13 = (s32[48]{0:T(128)S(1)}, s32[48]{0:T(128)}, u32[]{:S(2)}) copy-start(s32[48]{0:T(128)} %constant.113) | copy-start | bytes 580
  50.8 2.2 %copy-start.1 = (s32[16]{0:T(128)S(1)}, s32[16]{0:T(128)}, u32[]{:S(2)}) copy-start(s32[16]{0:T(128)} %param.29) | copy-start | bytes 196
  50.8 1.2 copy-start.5
  52.1 144.5 %all-reduce.3.cloned.1.call-start = ((), (), s32[]{:S(2)}) async-start(), calls=%async_computation.1 | async-start | bytes 3145728
  52.2 40.7 %copy-start.4 = (bf16[512,512]{1,0:T(8,128)(2,1)S(1)}, bf16[512,512]{1,0:T(8,128)(2,1)}, u32[]{:S(2)}) copy-start(bf16[512,512]{1,0:T(8,128)(2,1)} %param.22) | copy-start | bytes 1572868
  52.2 40.7 %copy-start.12 = (f32[512]{0:T(512)S(1)}, f32[512]{0:T(512)}, u32[]{:S(2)}) copy-start(f32[512]{0:T(512)} %param.23) | copy-start | bytes 6148
  90.5 3.4 %copy-start.2 = (bf16[64,16,512]{2,1,0:T(8,128)(2,1)S(1)}, bf16[64,16,512]{2,1,0:T(8,128)(2,1)}, u32[]{:S(2)}) copy-start(bf16[64,16,512]{2,1,0:T(8,128)(2,1)} %param.27) | copy-start | bytes 3145732
  101.9 0.8 copy-start.3
  101.9 1.0 copy-start.6
  101.9 1.0 copy-start.11
  102.7 1.3 copy-start.14
Sparse Core Ops, SparseCore 0:
  52.2 38.2 all-gather.3
  102.1 94.4 all-reduce.2
